TPU v7x, 32 devices: a whole 2x2x4 slice. The times are simulated.
32 devices in a mesh: gx: 4 (over z), gy: 8 (over y, x, core).
Axes of the slice: x: 2, y: 2, z: 4, core: 2. Of those that a mesh axis runs over, the one named last changes fastest.
Arguments:
- orbitals: bfloat16 [24, 48, 11, 256], P('gx', 'gy'), may hold values from -140 to 140, as said below
- masses: float32 [24, 48, 11], P('gx', 'gy'), may hold values from 0.5 to 2, as said below
- cell_matrices: bfloat16 [4, 8, 2, 216, 216], P('gx', 'gy'), may hold values from -0.12 to 3.12, as said below
Outputs:
- filtered_orbitals: bfloat16 [24, 48, 11, 256], P('gx', 'gy')
Inputs may be any that keep to these rules, and one draw needn't show every extreme that they name: Entries of orbitals that hold the same mesh node are equal. Entries of masses that hold the same mesh node are equal. `cell_matrices`: every cell matrix is symmetric.
All inputs are finite; a program needn't handle non-finite values.
Results may differ from a plain program's by a relative error of at most 0.0063.
The roundings to bfloat16 on the way count: a program that leaves them out, or rounds other values in their place, can miss the bound.
Values sent between devices are 32-bit elements; how exact they have to be, the bound alone decides.
A program may use at most 64 MiB of HBM per device.

v0:
```python
import jax
import jax.numpy as jnp
from jax import lax
from jax.sharding import PartitionSpec as P

FILTER_DEG = 3
NS_STEPS = 2
center_shift = 12.0
half_span = 12.0


def with_halo(array, sides, width):
    for axis, dim in sides:
        size, length = (lax.axis_size(axis), array.shape[dim])
        up = [(i, (i + 1) % size) for i in range(size)]
        down = [(j, i) for i, j in up]
        last = lax.slice_in_dim(array, length - width, length, axis=dim)
        leading = lax.slice_in_dim(array, 0, width, axis=dim)
        before = lax.ppermute(last, axis, up)
        after = lax.ppermute(leading, axis, down)
        array = jnp.concatenate([before, array, after], axis=dim)
    return array


def unfold_cells(values, along_dim, cells_along):
    moved = jnp.moveaxis(values, along_dim, 0)
    trailing = moved.shape[1:]
    main_part = moved[: 5 * cells_along].reshape((cells_along, 5) + trailing)
    far_layer = moved[5::5][:, None]
    window = jnp.concatenate([main_part, far_layer], 1)
    return jnp.moveaxis(window, (0, 1), (along_dim, along_dim + 1))


def fold_cells(window, along_dim, cells_along):
    moved = jnp.moveaxis(window, (along_dim, along_dim + 1), (0, 1))
    trailing = moved.shape[2:]
    leading = jnp.concatenate([moved[:, :5], jnp.zeros((1, 5) + trailing, moved.dtype)], 0)
    carried = jnp.concatenate([jnp.zeros((1,) + trailing, moved.dtype), moved[:, 5]], 0)
    leading = leading.at[:, 0].add(carried)
    flattened = leading.reshape((5 * (cells_along + 1),) + trailing)[: 5 * cells_along + 1]
    return jnp.moveaxis(flattened, 0, along_dim)


def to_cells(values, cells_x, cells_y, cells_z):
    window = unfold_cells(values, 0, cells_x)
    window = unfold_cells(window, 2, cells_y)
    window = unfold_cells(window, 4, cells_z)
    window = jnp.transpose(window, (0, 2, 4, 1, 3, 5, 6))
    return window.reshape((cells_x, cells_y, cells_z, 216, window.shape[-1]))


def from_cells(products, cells_x, cells_y, cells_z):
    window = products.reshape((cells_x, cells_y, cells_z, 6, 6, 6, products.shape[-1]))
    window = jnp.transpose(window, (0, 3, 1, 4, 2, 5, 6))
    window = fold_cells(window, 4, cells_z)
    window = fold_cells(window, 2, cells_y)
    return fold_cells(window, 0, cells_x)


def inverse_root(intersection):
    frob_norm = jnp.sqrt(jnp.sum(intersection * intersection))
    current = intersection / frob_norm
    identity = jnp.eye(intersection.shape[0], dtype=jnp.float32)
    factor_z = identity
    for sweep_index in range(NS_STEPS):
        step_t = 1.5 * identity - 0.5 * jnp.dot(factor_z, current, precision=lax.Precision.HIGHEST)
        current = jnp.dot(current, step_t, precision=lax.Precision.HIGHEST)
        factor_z = jnp.dot(step_t, factor_z, precision=lax.Precision.HIGHEST)
    return factor_z / jnp.sqrt(frob_norm)


def body(orbitals, masses, cell_matrices):
    cells_x, cells_y, cells_z = cell_matrices.shape[:3]
    orb_count = orbitals.shape[3]

    def apply_operator(rounded):
        cell_vectors = to_cells(rounded, cells_x, cells_y, cells_z)
        products = jnp.einsum(
            "abcij,abcjo->abcio", cell_matrices, cell_vectors, preferred_element_type=jnp.float32
        )
        partial_value = from_cells(products, cells_x, cells_y, cells_z)
        padded = with_halo(partial_value, (("gx", 0), ("gy", 1)), 1)
        summed = partial_value.at[0].add(padded[0, 1:-1]).at[-1].add(padded[-1, 1:-1])
        summed = summed.at[:, 0].add(padded[1:-1, 0]).at[:, -1].add(padded[1:-1, -1])
        summed = summed.at[0, 0].add(padded[0, 0]).at[0, -1].add(padded[0, -1])
        summed = summed.at[-1, 0].add(padded[-1, 0]).at[-1, -1].add(padded[-1, -1])
        return summed / masses[..., None]

    starting = orbitals.astype(jnp.float32)
    previous = starting
    current = (apply_operator(orbitals) - center_shift * starting) / half_span
    for sweep_index in range(FILTER_DEG - 1):
        following = (
            2.0
            * (apply_operator(current.astype(jnp.bfloat16)) - center_shift * current)
            / half_span
            - previous
        )
        previous = current
        current = following
    owned_rows = current[:-1, :-1].reshape((-1, orb_count))
    owned_mass = masses[:-1, :-1].reshape((-1, 1))
    local_intersection = jnp.einsum(
        "no,np->op", owned_rows * owned_mass, owned_rows, precision=lax.Precision.HIGHEST
    )
    node_total = (
        (current.shape[0] - 1)
        * lax.axis_size("gx")
        * (current.shape[1] - 1)
        * lax.axis_size("gy")
        * current.shape[2]
    )
    row_sum = lax.psum(local_intersection, "gy")
    intersection_sum = lax.psum(row_sum, "gx")
    intersection = intersection_sum / node_total
    factor = inverse_root(intersection)
    node_rows = current.reshape((-1, orb_count))
    result = jnp.dot(node_rows, factor, precision=lax.Precision.HIGHEST).astype(jnp.bfloat16)
    return result.reshape(current.shape)


def solution(mesh):
    return jax.shard_map(
        body,
        mesh=mesh,
        in_specs=(P("gx", "gy", None, None), P("gx", "gy", None), P("gx", "gy", None, None, None)),
        out_specs=P("gx", "gy", None, None),
        check_vma=False,
    )
```

profile of v0, /device:TPU:0, one launch (start us, length us, event | category | flops | bytes accessed | tf_op | source)
XLA Modules:
  0.0 195.6 jit_solution(4431525838171367299)
XLA Ops:
  6.5 1.0 copy-done.1
  14.5 3.1 %collective-permute-start = (f32[1,6,11,256]{3,2,1,0:T(8,128)S(1)}, f32[1,6,11,256]{3,2,1,0:T(8,128)S(1)}, u32[]{:S(2)}, u32[]{:S(2)}) collective-permute-start(f32[1,6,11,256]{3,2,1,0:T(8,128)S(1)} %slice.1363), channel_id=1, source_target_pairs={{0,8},{8,16},{16,24},{24,0},{1,9},{9,17},{17,25},{25,1},{2,10},{10... | collective-permute-start | bytes 202760 | tf_op jit(solution)/shard_map/ppermute | solution.py:19
  19.0 3.4 %collective-permute-done = f32[1,6,11,256]{3,2,1,0:T(8,128)S(1)} collective-permute-done((f32[1,6,11,256]{3,2,1,0:T(8,128)S(1)}, f32[1,6,11,256]{3,2,1,0:T(8,128)S(1)}, u32[]{:S(2)}, u32[]{:S(2)}) %collective-permute-start) | collective-permute-done | bytes 67616 | tf_op jit(solution)/shard_map/ppermute | solution.py:19
  22.4 1.9 collective-permute-start.1
  24.8 2.2 %collective-permute-done.1 = f32[1,6,11,256]{3,2,1,0:T(8,128)S(1)} collective-permute-done((f32[1,6,11,256]{3,2,1,0:T(8,128)S(1)}, f32[1,6,11,256]{3,2,1,0:T(8,128)S(1)}, u32[]{:S(2)}, u32[]{:S(2)}) %collective-permute-start.1) | collective-permute-done | bytes 67616 | tf_op jit(solution)/shard_map/ppermute | solution.py:20
  27.1 2.6 %collective-permute-start.3 = (f32[8,1,11,256]{3,2,1,0:T(8,128)S(1)}, f32[8,1,11,256]{3,2,1,0:T(8,128)S(1)}, u32[]{:S(2)}, u32[]{:S(2)}) collective-permute-start(f32[8,1,11,256]{3,2,1,0:T(8,128)S(1)} %get-tuple-element.411), channel_id=1, source_target_pairs={{1,0},{2,1},{3,2},{4,3},{5,4},{6,5},{7,6},{0,7},{9,8},{10,9},{11,1... | collective-permute-start | bytes 270344 | tf_op jit(solution)/shard_map/ppermute | solution.py:20
  29.8 2.6 %collective-permute-done.2 = f32[8,1,11,256]{3,2,1,0:T(8,128)S(1)} collective-permute-done((f32[8,1,11,256]{3,2,1,0:T(8,128)S(1)}, f32[8,1,11,256]{3,2,1,0:T(8,128)S(1)}, u32[]{:S(2)}, u32[]{:S(2)}) %collective-permute-start.2) | collective-permute-done | bytes 90144 | tf_op jit(solution)/shard_map/ppermute | solution.py:19
  32.5 1.9 fusion.32
  42.3 7.1 %collective-permute-done.4 = f32[1,6,11,256]{3,2,1,0:T(8,128)S(1)} collective-permute-done((f32[1,6,11,256]{3,2,1,0:T(8,128)S(1)}, f32[1,6,11,256]{3,2,1,0:T(8,128)S(1)}, u32[]{:S(2)}, u32[]{:S(2)}) %collective-permute-start.4) | collective-permute-done | bytes 67616 | tf_op jit(solution)/shard_map/ppermute | solution.py:19
  49.4 1.9 collective-permute-start.5
  51.3 3.0 %collective-permute-done.5 = f32[1,6,11,256]{3,2,1,0:T(8,128)S(1)} collective-permute-done((f32[1,6,11,256]{3,2,1,0:T(8,128)S(1)}, f32[1,6,11,256]{3,2,1,0:T(8,128)S(1)}, u32[]{:S(2)}, u32[]{:S(2)}) %collective-permute-start.5) | collective-permute-done | bytes 67616 | tf_op jit(solution)/shard_map/ppermute | solution.py:20
  54.4 2.6 %collective-permute-start.7 = (f32[8,1,11,256]{3,2,1,0:T(8,128)S(1)}, f32[8,1,11,256]{3,2,1,0:T(8,128)S(1)}, u32[]{:S(2)}, u32[]{:S(2)}) collective-permute-start(f32[8,1,11,256]{3,2,1,0:T(8,128)S(1)} %get-tuple-element.409), channel_id=1, source_target_pairs={{1,0},{2,1},{3,2},{4,3},{5,4},{6,5},{7,6},{0,7},{9,8},{10,9},{11,1... | collective-permute-start | bytes 270344 | tf_op jit(solution)/shard_map/ppermute | solution.py:20
  57.0 3.1 %collective-permute-done.6 = f32[8,1,11,256]{3,2,1,0:T(8,128)S(1)} collective-permute-done((f32[8,1,11,256]{3,2,1,0:T(8,128)S(1)}, f32[8,1,11,256]{3,2,1,0:T(8,128)S(1)}, u32[]{:S(2)}, u32[]{:S(2)}) %collective-permute-start.6) | collective-permute-done | bytes 90144 | tf_op jit(solution)/shard_map/ppermute | solution.py:19
  60.2 1.9 fusion.33
  69.4 7.0 %collective-permute-done.8 = f32[1,6,11,256]{3,2,1,0:T(8,128)S(1)} collective-permute-done((f32[1,6,11,256]{3,2,1,0:T(8,128)S(1)}, f32[1,6,11,256]{3,2,1,0:T(8,128)S(1)}, u32[]{:S(2)}, u32[]{:S(2)}) %collective-permute-start.8) | collective-permute-done | bytes 67616 | tf_op jit(solution)/shard_map/ppermute | solution.py:19
  76.3 2.0 %collective-permute-start.9 = (f32[1,6,11,256]{3,2,1,0:T(8,128)S(1)}, f32[1,6,11,256]{3,2,1,0:T(8,128)S(1)}, u32[]{:S(2)}, u32[]{:S(2)}) collective-permute-start(f32[1,6,11,256]{3,2,1,0:T(8,128)S(1)} %get-tuple-element.401), channel_id=1, source_target_pairs={{8,0},{16,8},{24,16},{0,24},{9,1},{17,9},{25,17},{1,25},{10,2},{18... | collective-permute-start | bytes 202760 | tf_op jit(solution)/shard_map/ppermute | solution.py:20
  78.4 2.9 %collective-permute-done.9 = f32[1,6,11,256]{3,2,1,0:T(8,128)S(1)} collective-permute-done((f32[1,6,11,256]{3,2,1,0:T(8,128)S(1)}, f32[1,6,11,256]{3,2,1,0:T(8,128)S(1)}, u32[]{:S(2)}, u32[]{:S(2)}) %collective-permute-start.9) | collective-permute-done | bytes 67616 | tf_op jit(solution)/shard_map/ppermute | solution.py:20
  81.3 2.6 %collective-permute-start.11 = (f32[8,1,11,256]{3,2,1,0:T(8,128)S(1)}, f32[8,1,11,256]{3,2,1,0:T(8,128)S(1)}, u32[]{:S(2)}, u32[]{:S(2)}) collective-permute-start(f32[8,1,11,256]{3,2,1,0:T(8,128)S(1)} %get-tuple-element.407), channel_id=1, source_target_pairs={{1,0},{2,1},{3,2},{4,3},{5,4},{6,5},{7,6},{0,7},{9,8},{10,9},{11,1... | collective-permute-start | bytes 270344 | tf_op jit(solution)/shard_map/ppermute | solution.py:20
  84.0 3.9 %collective-permute-done.10 = f32[8,1,11,256]{3,2,1,0:T(8,128)S(1)} collective-permute-done((f32[8,1,11,256]{3,2,1,0:T(8,128)S(1)}, f32[8,1,11,256]{3,2,1,0:T(8,128)S(1)}, u32[]{:S(2)}, u32[]{:S(2)}) %collective-permute-start.10) | collective-permute-done | bytes 90144 | tf_op jit(solution)/shard_map/ppermute | solution.py:19
  87.9 1.9 fusion.34
  90.3 1.9 convolution_bitcast_fusion.3
  92.2 53.8 %all-reduce.21.cloned.1.call-done = f32[256,256]{1,0:T(8,128)} async-done(((f32[256,256]{1,0:T(8,128)}), f32[256,256]{1,0:T(8,128)}) %all-reduce.21.cloned.1.call-update) | async-done | bytes 262160 | tf_op jit(solution)/shard_map/psum | solution.py:113
  146.1 37.1 %all-reduce.23.cloned.1.call-done = f32[256,256]{1,0:T(8,128)} async-done(((f32[256,256]{1,0:T(8,128)}), f32[256,256]{1,0:T(8,128)}) %all-reduce.23.cloned.1.call-update) | async-done | bytes 262160 | tf_op jit(solution)/shard_map/psum | solution.py:114
  183.2 1.7 multiply_reduce_fusion
  (184 shorter events, 27.3 us)
Async XLA Ops:
  6.5 2.0 %copy-start = (bf16[1,1,2,216,216]{4,3,2,1,0:T(8,128)(2,1)S(1)}, bf16[1,1,2,216,216]{4,3,2,1,0:T(8,128)(2,1)}, u32[]{:S(2)}) copy-start(bf16[1,1,2,216,216]{4,3,2,1,0:T(8,128)(2,1)} %param.71) | copy-start | bytes 559876
  6.5 1.0 copy-start.1
  6.5 1.1 slice-start
  6.5 139.5 %all-reduce.21.cloned.1.call-start = ((), (), s32[]{:S(2)}) async-start(), calls=%async_computation | async-start | bytes 524288 | tf_op jit(solution)/shard_map/psum | solution.py:113
  10.4 0.8 copy-start.2
  11.2 0.9 slice-start.1
  14.5 7.9 %collective-permute-start = (f32[1,6,11,256]{3,2,1,0:T(8,128)S(1)}, f32[1,6,11,256]{3,2,1,0:T(8,128)S(1)}, u32[]{:S(2)}, u32[]{:S(2)}) collective-permute-start(f32[1,6,11,256]{3,2,1,0:T(8,128)S(1)} %slice.1363), channel_id=1, source_target_pairs={{0,8},{8,16},{16,24},{24,0},{1,9},{9,17},{17,25},{25,1},{2,10},{10... | collective-permute-start | bytes 202760 | tf_op jit(solution)/shard_map/ppermute | solution.py:19
  22.4 4.7 %collective-permute-start.1 = (f32[1,6,11,256]{3,2,1,0:T(8,128)S(1)}, f32[1,6,11,256]{3,2,1,0:T(8,128)S(1)}, u32[]{:S(2)}, u32[]{:S(2)}) collective-permute-start(f32[1,6,11,256]{3,2,1,0:T(8,128)S(1)} %get-tuple-element.405), channel_id=1, source_target_pairs={{8,0},{16,8},{24,16},{0,24},{9,1},{17,9},{25,17},{1,25},{10,2},{18... | collective-permute-start | bytes 202760 | tf_op jit(solution)/shard_map/ppermute | solution.py:20
  27.1 5.3 %collective-permute-start.2 = (f32[8,1,11,256]{3,2,1,0:T(8,128)S(1)}, f32[8,1,11,256]{3,2,1,0:T(8,128)S(1)}, u32[]{:S(2)}, u32[]{:S(2)}) collective-permute-start(f32[8,1,11,256]{3,2,1,0:T(8,128)S(1)} %get-tuple-element.412), channel_id=1, source_target_pairs={{0,1},{1,2},{2,3},{3,4},{4,5},{5,6},{6,7},{7,0},{8,9},{9,10},{10,1... | collective-permute-start | bytes 270344 | tf_op jit(solution)/shard_map/ppermute | solution.py:19
  27.1 5.3 %collective-permute-start.3 = (f32[8,1,11,256]{3,2,1,0:T(8,128)S(1)}, f32[8,1,11,256]{3,2,1,0:T(8,128)S(1)}, u32[]{:S(2)}, u32[]{:S(2)}) collective-permute-start(f32[8,1,11,256]{3,2,1,0:T(8,128)S(1)} %get-tuple-element.411), channel_id=1, source_target_pairs={{1,0},{2,1},{3,2},{4,3},{5,4},{6,5},{7,6},{0,7},{9,8},{10,9},{11,1... | collective-permute-start | bytes 270344 | tf_op jit(solution)/shard_map/ppermute | solution.py:20
  38.1 0.8 copy-start.3
  38.9 0.9 slice-start.2
  42.1 7.3 %collective-permute-start.4 = (f32[1,6,11,256]{3,2,1,0:T(8,128)S(1)}, f32[1,6,11,256]{3,2,1,0:T(8,128)S(1)}, u32[]{:S(2)}, u32[]{:S(2)}) collective-permute-start(f32[1,6,11,256]{3,2,1,0:T(8,128)S(1)} %slice.1391), channel_id=1, source_target_pairs={{0,8},{8,16},{16,24},{24,0},{1,9},{9,17},{17,25},{25,1},{2,10},{10... | collective-permute-start | bytes 202760 | tf_op jit(solution)/shard_map/ppermute | solution.py:19
  49.4 4.9 %collective-permute-start.5 = (f32[1,6,11,256]{3,2,1,0:T(8,128)S(1)}, f32[1,6,11,256]{3,2,1,0:T(8,128)S(1)}, u32[]{:S(2)}, u32[]{:S(2)}) collective-permute-start(f32[1,6,11,256]{3,2,1,0:T(8,128)S(1)} %get-tuple-element.403), channel_id=1, source_target_pairs={{8,0},{16,8},{24,16},{0,24},{9,1},{17,9},{25,17},{1,25},{10,2},{18... | collective-permute-start | bytes 202760 | tf_op jit(solution)/shard_map/ppermute | solution.py:20
  54.3 5.8 %collective-permute-start.6 = (f32[8,1,11,256]{3,2,1,0:T(8,128)S(1)}, f32[8,1,11,256]{3,2,1,0:T(8,128)S(1)}, u32[]{:S(2)}, u32[]{:S(2)}) collective-permute-start(f32[8,1,11,256]{3,2,1,0:T(8,128)S(1)} %get-tuple-element.410), channel_id=1, source_target_pairs={{0,1},{1,2},{2,3},{3,4},{4,5},{5,6},{6,7},{7,0},{8,9},{9,10},{10,1... | collective-permute-start | bytes 270344 | tf_op jit(solution)/shard_map/ppermute | solution.py:19
  54.4 5.8 %collective-permute-start.7 = (f32[8,1,11,256]{3,2,1,0:T(8,128)S(1)}, f32[8,1,11,256]{3,2,1,0:T(8,128)S(1)}, u32[]{:S(2)}, u32[]{:S(2)}) collective-permute-start(f32[8,1,11,256]{3,2,1,0:T(8,128)S(1)} %get-tuple-element.409), channel_id=1, source_target_pairs={{1,0},{2,1},{3,2},{4,3},{5,4},{6,5},{7,6},{0,7},{9,8},{10,9},{11,1... | collective-permute-start | bytes 270344 | tf_op jit(solution)/shard_map/ppermute | solution.py:20
  65.2 0.8 copy-start.4
  65.9 0.9 slice-start.3
  69.2 7.1 %collective-permute-start.8 = (f32[1,6,11,256]{3,2,1,0:T(8,128)S(1)}, f32[1,6,11,256]{3,2,1,0:T(8,128)S(1)}, u32[]{:S(2)}, u32[]{:S(2)}) collective-permute-start(f32[1,6,11,256]{3,2,1,0:T(8,128)S(1)} %slice.1419), channel_id=1, source_target_pairs={{0,8},{8,16},{16,24},{24,0},{1,9},{9,17},{17,25},{25,1},{2,10},{10... | collective-permute-start | bytes 202760 | tf_op jit(solution)/shard_map/ppermute | solution.py:19
  76.3 4.9 %collective-permute-start.9 = (f32[1,6,11,256]{3,2,1,0:T(8,128)S(1)}, f32[1,6,11,256]{3,2,1,0:T(8,128)S(1)}, u32[]{:S(2)}, u32[]{:S(2)}) collective-permute-start(f32[1,6,11,256]{3,2,1,0:T(8,128)S(1)} %get-tuple-element.401), channel_id=1, source_target_pairs={{8,0},{16,8},{24,16},{0,24},{9,1},{17,9},{25,17},{1,25},{10,2},{18... | collective-permute-start | bytes 202760 | tf_op jit(solution)/shard_map/ppermute | solution.py:20
  81.3 6.6 %collective-permute-start.10 = (f32[8,1,11,256]{3,2,1,0:T(8,128)S(1)}, f32[8,1,11,256]{3,2,1,0:T(8,128)S(1)}, u32[]{:S(2)}, u32[]{:S(2)}) collective-permute-start(f32[8,1,11,256]{3,2,1,0:T(8,128)S(1)} %get-tuple-element.408), channel_id=1, source_target_pairs={{0,1},{1,2},{2,3},{3,4},{4,5},{5,6},{6,7},{7,0},{8,9},{9,10},{10,1... | collective-permute-start | bytes 270344 | tf_op jit(solution)/shard_map/ppermute | solution.py:19
  81.3 6.6 %collective-permute-start.11 = (f32[8,1,11,256]{3,2,1,0:T(8,128)S(1)}, f32[8,1,11,256]{3,2,1,0:T(8,128)S(1)}, u32[]{:S(2)}, u32[]{:S(2)}) collective-permute-start(f32[8,1,11,256]{3,2,1,0:T(8,128)S(1)} %get-tuple-element.407), channel_id=1, source_target_pairs={{1,0},{2,1},{3,2},{4,3},{5,4},{6,5},{7,6},{0,7},{9,8},{10,9},{11,1... | collective-permute-start | bytes 270344 | tf_op jit(solution)/shard_map/ppermute | solution.py:20
  92.2 91.0 %all-reduce.23.cloned.1.call-start = ((), (), s32[]{:S(2)}) async-start(), calls=%async_computation.1 | async-start | bytes 524288 | tf_op jit(solution)/shard_map/psum | solution.py:114
  183.2 2.4 %copy-start.6 = (f32[256,256]{1,0:T(8,128)S(1)}, f32[256,256]{1,0:T(8,128)}, u32[]{:S(2)}) copy-start(f32[256,256]{1,0:T(8,128)} %all-reduce.23.cloned.1.call-done) | copy-start | bytes 786436
  (2 other events, 1.4 us)
Sparse Core Ops, SparseCore 0:
  92.3 53.6 all-reduce.20
  148.4 34.6 all-reduce.22
where the time goes:
time: 196 us
  waiting for transfers between devices  126 us (64%)
  local copies, waits for them, and re-layouts  21 us (11%)
  starting transfers between devices  17.1 us (9%)
  between operations  15.3 us (8%)
  other arithmetic  11.6 us (6%)
  matrix products  4.74 us (2%)
    psum x1, waiting for transfers between devices, body(): row_sum = lax.psum(local_intersection, 'gy')  53.8 us
    psum x1, waiting for transfers between devices, body(): intersection_sum = lax.psum(row_sum, 'gx')  37.1 us
    ppermute x6, waiting for transfers between devices, with_halo(): before = lax.ppermute(last, axis, up)  27 us
    ppermute x6, starting transfers between devices, with_halo(): after = lax.ppermute(leading, axis, down)  13.6 us
    ppermute x6, waiting for transfers between devices, with_halo(): after = lax.ppermute(leading, axis, down)  8.1 us
    scatter-add x6, other arithmetic, apply_operator(): summed = summed.at[0, 0].add(padded[0, 0]).at[0, -1].add(padded[0, -1])  5.81 us
    unnamed x26, local copies, waits for them, and re-layouts  5.14 us
    scatter-add x9, local copies, waits for them, and re-layouts, fold_cells(): leading = leading.at[:, 0].add(carried)  4.14 us
  transfers between devices with their start and end apart: 14, of which 11 were waited for; matrix products, arithmetic and copies ran while one was open for 1% of the time, Pallas kernels for 0%

commit v1 on v0

--- a/solution.py
+++ b/solution.py
@@ -111,7 +111,7 @@
         * current.shape[2]
     )
     row_sum = lax.psum(local_intersection, "gy")
-    intersection_sum = lax.psum(row_sum, "gx")
+    intersection_sum = jnp.sum(lax.all_gather(row_sum, "gx"), axis=0)
     intersection = intersection_sum / node_total
     factor = inverse_root(intersection)
     node_rows = current.reshape((-1, orb_count))

time: 196 us -> 188 us (0.959)
  waiting for transfers between devices: 126 us -> 118 us
    psum x1 -> x0, waiting for transfers between devices: 37.1 us -> none  [body(): intersection_sum = lax.psum(row_sum, 'gx')]
    all_gather x0 -> x1, waiting for transfers between devices: none -> 28.9 us  [body(): intersection_sum = jnp.sum(lax.all_gather(row_sum, 'gx'), axis=0)]
    unnamed x26 -> x24, local copies, waits for them, and re-layouts: 5.14 us -> 5.13 us
where the time goes in v1:
time: 188 us
  waiting for transfers between devices  118 us (63%)
  local copies, waits for them, and re-layouts  20.9 us (11%)
  starting transfers between devices  17.1 us (9%)
  between operations  15.3 us (8%)
  other arithmetic  11.8 us (6%)
  matrix products  4.73 us (3%)
    psum x1, waiting for transfers between devices, body(): row_sum = lax.psum(local_intersection, 'gy')  53.8 us
    all_gather x1, waiting for transfers between devices, body(): intersection_sum = jnp.sum(lax.all_gather(row_sum, 'gx'), axis=0)  28.9 us
    ppermute x6, waiting for transfers between devices, with_halo(): before = lax.ppermute(last, axis, up)  27 us
    ppermute x6, starting transfers between devices, with_halo(): after = lax.ppermute(leading, axis, down)  13.6 us
    ppermute x6, waiting for transfers between devices, with_halo(): after = lax.ppermute(leading, axis, down)  8.1 us
    scatter-add x6, other arithmetic, apply_operator(): summed = summed.at[0, 0].add(padded[0, 0]).at[0, -1].add(padded[0, -1])  5.67 us
    unnamed x24, local copies, waits for them, and re-layouts  5.13 us
    scatter-add x9, local copies, waits for them, and re-layouts, fold_cells(): leading = leading.at[:, 0].add(carried)  4.14 us
  transfers between devices with their start and end apart: 14, of which 11 were waited for; matrix products, arithmetic and copies ran while one was open for 1% of the time, Pallas kernels for 0%

profile of v1, /device:TPU:0, one launch (start us, length us, event | category | flops | bytes accessed | tf_op | source)
XLA Modules:
  0.0 187.6 jit_solution(2126964210829399947)
XLA Ops:
  6.5 1.0 copy-done.1
  14.5 3.1 %collective-permute-start = (f32[1,6,11,256]{3,2,1,0:T(8,128)S(1)}, f32[1,6,11,256]{3,2,1,0:T(8,128)S(1)}, u32[]{:S(2)}, u32[]{:S(2)}) collective-permute-start(f32[1,6,11,256]{3,2,1,0:T(8,128)S(1)} %slice.1363), channel_id=1, source_target_pairs={{0,8},{8,16},{16,24},{24,0},{1,9},{9,17},{17,25},{25,1},{2,10},{10... | collective-permute-start | bytes 202760 | tf_op jit(solution)/shard_map/ppermute | solution.py:19
  19.0 3.3 %collective-permute-done = f32[1,6,11,256]{3,2,1,0:T(8,128)S(1)} collective-permute-done((f32[1,6,11,256]{3,2,1,0:T(8,128)S(1)}, f32[1,6,11,256]{3,2,1,0:T(8,128)S(1)}, u32[]{:S(2)}, u32[]{:S(2)}) %collective-permute-start) | collective-permute-done | bytes 67616 | tf_op jit(solution)/shard_map/ppermute | solution.py:19
  22.4 1.9 collective-permute-start.1
  24.8 2.2 %collective-permute-done.1 = f32[1,6,11,256]{3,2,1,0:T(8,128)S(1)} collective-permute-done((f32[1,6,11,256]{3,2,1,0:T(8,128)S(1)}, f32[1,6,11,256]{3,2,1,0:T(8,128)S(1)}, u32[]{:S(2)}, u32[]{:S(2)}) %collective-permute-start.1) | collective-permute-done | bytes 67616 | tf_op jit(solution)/shard_map/ppermute | solution.py:20
  27.1 2.6 %collective-permute-start.3 = (f32[8,1,11,256]{3,2,1,0:T(8,128)S(1)}, f32[8,1,11,256]{3,2,1,0:T(8,128)S(1)}, u32[]{:S(2)}, u32[]{:S(2)}) collective-permute-start(f32[8,1,11,256]{3,2,1,0:T(8,128)S(1)} %get-tuple-element.411), channel_id=1, source_target_pairs={{1,0},{2,1},{3,2},{4,3},{5,4},{6,5},{7,6},{0,7},{9,8},{10,9},{11,1... | collective-permute-start | bytes 270344 | tf_op jit(solution)/shard_map/ppermute | solution.py:20
  29.8 2.6 %collective-permute-done.2 = f32[8,1,11,256]{3,2,1,0:T(8,128)S(1)} collective-permute-done((f32[8,1,11,256]{3,2,1,0:T(8,128)S(1)}, f32[8,1,11,256]{3,2,1,0:T(8,128)S(1)}, u32[]{:S(2)}, u32[]{:S(2)}) %collective-permute-start.2) | collective-permute-done | bytes 90144 | tf_op jit(solution)/shard_map/ppermute | solution.py:19
  32.5 1.9 %fusion.32 = f32[6,6,11,256]{3,2,1,0:T(8,128)S(1)} fusion(f32[6,6,11,256]{3,2,1,0:T(8,128)S(1)} %fusion.43, s32[]{:T(128)} %bitcast.27, s32[]{:T(128)} %bitcast.28, f32[8,1,11,256]{3,2,1,0:T(8,128)S(1)} %collective-permute-done.3, pred[]{:T(512)} %and_reduce_fusion), kind=kLoop, calls=%fused_computation.117 | loop fusion | flops 5632 | bytes 49161 | tf_op jit(solution)/shard_map/scatter-add | solution.py:85
  42.2 7.1 %collective-permute-done.4 = f32[1,6,11,256]{3,2,1,0:T(8,128)S(1)} collective-permute-done((f32[1,6,11,256]{3,2,1,0:T(8,128)S(1)}, f32[1,6,11,256]{3,2,1,0:T(8,128)S(1)}, u32[]{:S(2)}, u32[]{:S(2)}) %collective-permute-start.4) | collective-permute-done | bytes 67616 | tf_op jit(solution)/shard_map/ppermute | solution.py:19
  49.3 1.9 collective-permute-start.5
  51.2 3.0 %collective-permute-done.5 = f32[1,6,11,256]{3,2,1,0:T(8,128)S(1)} collective-permute-done((f32[1,6,11,256]{3,2,1,0:T(8,128)S(1)}, f32[1,6,11,256]{3,2,1,0:T(8,128)S(1)}, u32[]{:S(2)}, u32[]{:S(2)}) %collective-permute-start.5) | collective-permute-done | bytes 67616 | tf_op jit(solution)/shard_map/ppermute | solution.py:20
  54.3 2.6 %collective-permute-start.7 = (f32[8,1,11,256]{3,2,1,0:T(8,128)S(1)}, f32[8,1,11,256]{3,2,1,0:T(8,128)S(1)}, u32[]{:S(2)}, u32[]{:S(2)}) collective-permute-start(f32[8,1,11,256]{3,2,1,0:T(8,128)S(1)} %get-tuple-element.409), channel_id=1, source_target_pairs={{1,0},{2,1},{3,2},{4,3},{5,4},{6,5},{7,6},{0,7},{9,8},{10,9},{11,1... | collective-permute-start | bytes 270344 | tf_op jit(solution)/shard_map/ppermute | solution.py:20
  57.0 3.1 %collective-permute-done.6 = f32[8,1,11,256]{3,2,1,0:T(8,128)S(1)} collective-permute-done((f32[8,1,11,256]{3,2,1,0:T(8,128)S(1)}, f32[8,1,11,256]{3,2,1,0:T(8,128)S(1)}, u32[]{:S(2)}, u32[]{:S(2)}) %collective-permute-start.6) | collective-permute-done | bytes 90144 | tf_op jit(solution)/shard_map/ppermute | solution.py:19
  60.2 1.9 %fusion.33 = f32[6,6,11,256]{3,2,1,0:T(8,128)S(1)} fusion(f32[6,6,11,256]{3,2,1,0:T(8,128)S(1)} %fusion.40, s32[]{:T(128)} %bitcast.27, s32[]{:T(128)} %bitcast.28, f32[8,1,11,256]{3,2,1,0:T(8,128)S(1)} %collective-permute-done.7, pred[]{:T(512)} %and_reduce_fusion), kind=kLoop, calls=%fused_computation.118 | loop fusion | flops 5632 | bytes 49161 | tf_op jit(solution)/shard_map/scatter-add | solution.py:85
  69.2 7.0 %collective-permute-done.8 = f32[1,6,11,256]{3,2,1,0:T(8,128)S(1)} collective-permute-done((f32[1,6,11,256]{3,2,1,0:T(8,128)S(1)}, f32[1,6,11,256]{3,2,1,0:T(8,128)S(1)}, u32[]{:S(2)}, u32[]{:S(2)}) %collective-permute-start.8) | collective-permute-done | bytes 67616 | tf_op jit(solution)/shard_map/ppermute | solution.py:19
  76.2 2.0 %collective-permute-start.9 = (f32[1,6,11,256]{3,2,1,0:T(8,128)S(1)}, f32[1,6,11,256]{3,2,1,0:T(8,128)S(1)}, u32[]{:S(2)}, u32[]{:S(2)}) collective-permute-start(f32[1,6,11,256]{3,2,1,0:T(8,128)S(1)} %get-tuple-element.401), channel_id=1, source_target_pairs={{8,0},{16,8},{24,16},{0,24},{9,1},{17,9},{25,17},{1,25},{10,2},{18... | collective-permute-start | bytes 202760 | tf_op jit(solution)/shard_map/ppermute | solution.py:20
  78.3 2.9 %collective-permute-done.9 = f32[1,6,11,256]{3,2,1,0:T(8,128)S(1)} collective-permute-done((f32[1,6,11,256]{3,2,1,0:T(8,128)S(1)}, f32[1,6,11,256]{3,2,1,0:T(8,128)S(1)}, u32[]{:S(2)}, u32[]{:S(2)}) %collective-permute-start.9) | collective-permute-done | bytes 67616 | tf_op jit(solution)/shard_map/ppermute | solution.py:20
  81.2 2.6 %collective-permute-start.11 = (f32[8,1,11,256]{3,2,1,0:T(8,128)S(1)}, f32[8,1,11,256]{3,2,1,0:T(8,128)S(1)}, u32[]{:S(2)}, u32[]{:S(2)}) collective-permute-start(f32[8,1,11,256]{3,2,1,0:T(8,128)S(1)} %get-tuple-element.407), channel_id=1, source_target_pairs={{1,0},{2,1},{3,2},{4,3},{5,4},{6,5},{7,6},{0,7},{9,8},{10,9},{11,1... | collective-permute-start | bytes 270344 | tf_op jit(solution)/shard_map/ppermute | solution.py:20
  83.9 3.9 %collective-permute-done.10 = f32[8,1,11,256]{3,2,1,0:T(8,128)S(1)} collective-permute-done((f32[8,1,11,256]{3,2,1,0:T(8,128)S(1)}, f32[8,1,11,256]{3,2,1,0:T(8,128)S(1)}, u32[]{:S(2)}, u32[]{:S(2)}) %collective-permute-start.10) | collective-permute-done | bytes 90144 | tf_op jit(solution)/shard_map/ppermute | solution.py:19
  87.8 1.9 %fusion.34 = f32[6,6,11,256]{3,2,1,0:T(8,128)S(1)} fusion(f32[6,6,11,256]{3,2,1,0:T(8,128)S(1)} %fusion.37, s32[]{:T(128)} %bitcast.27, s32[]{:T(128)} %bitcast.28, f32[8,1,11,256]{3,2,1,0:T(8,128)S(1)} %collective-permute-done.11, pred[]{:T(512)} %and_reduce_fusion), kind=kLoop, calls=%fused_computation.119 | loop fusion | flops 5632 | bytes 49161 | tf_op jit(solution)/shard_map/scatter-add | solution.py:85
  90.1 1.9 convolution_bitcast_fusion.3
  92.1 53.8 %all-reduce.20.cloned.1.call-done = f32[1,256,256]{2,1,0:T(8,128)} async-done(((f32[1,256,256]{2,1,0:T(8,128)}), f32[1,256,256]{2,1,0:T(8,128)}) %all-reduce.20.cloned.1.call-update) | async-done | bytes 262160 | tf_op jit(solution)/shard_map/psum | solution.py:113
  146.0 28.9 %all-gather.2.cloned.1.call-done = f32[4,256,256]{2,1,0:T(8,128)} async-done(((f32[1,256,256]{2,1,0:T(8,128)}), f32[4,256,256]{2,1,0:T(8,128)}) %all-gather.2.cloned.1.call-update) | async-done | bytes 1048592 | tf_op jit(solution)/shard_map/all_gather | solution.py:114
  174.8 1.3 reduce_sum.18
  (183 shorter events, 28.0 us)
Async XLA Ops:
  6.5 2.0 %copy-start = (bf16[1,1,2,216,216]{4,3,2,1,0:T(8,128)(2,1)S(1)}, bf16[1,1,2,216,216]{4,3,2,1,0:T(8,128)(2,1)}, u32[]{:S(2)}) copy-start(bf16[1,1,2,216,216]{4,3,2,1,0:T(8,128)(2,1)} %param.71) | copy-start | bytes 559876
  6.5 1.0 copy-start.1
  6.5 1.1 slice-start
  6.5 139.3 %all-reduce.20.cloned.1.call-start = ((), (), s32[]{:S(2)}) async-start(), calls=%async_computation | async-start | bytes 524288 | tf_op jit(solution)/shard_map/psum | solution.py:113
  10.4 0.8 copy-start.2
  11.2 0.9 slice-start.1
  14.5 7.9 %collective-permute-start = (f32[1,6,11,256]{3,2,1,0:T(8,128)S(1)}, f32[1,6,11,256]{3,2,1,0:T(8,128)S(1)}, u32[]{:S(2)}, u32[]{:S(2)}) collective-permute-start(f32[1,6,11,256]{3,2,1,0:T(8,128)S(1)} %slice.1363), channel_id=1, source_target_pairs={{0,8},{8,16},{16,24},{24,0},{1,9},{9,17},{17,25},{25,1},{2,10},{10... | collective-permute-start | bytes 202760 | tf_op jit(solution)/shard_map/ppermute | solution.py:19
  22.4 4.7 %collective-permute-start.1 = (f32[1,6,11,256]{3,2,1,0:T(8,128)S(1)}, f32[1,6,11,256]{3,2,1,0:T(8,128)S(1)}, u32[]{:S(2)}, u32[]{:S(2)}) collective-permute-start(f32[1,6,11,256]{3,2,1,0:T(8,128)S(1)} %get-tuple-element.405), channel_id=1, source_target_pairs={{8,0},{16,8},{24,16},{0,24},{9,1},{17,9},{25,17},{1,25},{10,2},{18... | collective-permute-start | bytes 202760 | tf_op jit(solution)/shard_map/ppermute | solution.py:20
  27.1 5.3 %collective-permute-start.2 = (f32[8,1,11,256]{3,2,1,0:T(8,128)S(1)}, f32[8,1,11,256]{3,2,1,0:T(8,128)S(1)}, u32[]{:S(2)}, u32[]{:S(2)}) collective-permute-start(f32[8,1,11,256]{3,2,1,0:T(8,128)S(1)} %get-tuple-element.412), channel_id=1, source_target_pairs={{0,1},{1,2},{2,3},{3,4},{4,5},{5,6},{6,7},{7,0},{8,9},{9,10},{10,1... | collective-permute-start | bytes 270344 | tf_op jit(solution)/shard_map/ppermute | solution.py:19
  27.1 5.3 %collective-permute-start.3 = (f32[8,1,11,256]{3,2,1,0:T(8,128)S(1)}, f32[8,1,11,256]{3,2,1,0:T(8,128)S(1)}, u32[]{:S(2)}, u32[]{:S(2)}) collective-permute-start(f32[8,1,11,256]{3,2,1,0:T(8,128)S(1)} %get-tuple-element.411), channel_id=1, source_target_pairs={{1,0},{2,1},{3,2},{4,3},{5,4},{6,5},{7,6},{0,7},{9,8},{10,9},{11,1... | collective-permute-start | bytes 270344 | tf_op jit(solution)/shard_map/ppermute | solution.py:20
  34.4 0.7 copy-start.5
  38.0 0.8 copy-start.3
  38.8 0.9 slice-start.2
  42.1 7.3 %collective-permute-start.4 = (f32[1,6,11,256]{3,2,1,0:T(8,128)S(1)}, f32[1,6,11,256]{3,2,1,0:T(8,128)S(1)}, u32[]{:S(2)}, u32[]{:S(2)}) collective-permute-start(f32[1,6,11,256]{3,2,1,0:T(8,128)S(1)} %slice.1391), channel_id=1, source_target_pairs={{0,8},{8,16},{16,24},{24,0},{1,9},{9,17},{17,25},{25,1},{2,10},{10... | collective-permute-start | bytes 202760 | tf_op jit(solution)/shard_map/ppermute | solution.py:19
  49.3 4.9 %collective-permute-start.5 = (f32[1,6,11,256]{3,2,1,0:T(8,128)S(1)}, f32[1,6,11,256]{3,2,1,0:T(8,128)S(1)}, u32[]{:S(2)}, u32[]{:S(2)}) collective-permute-start(f32[1,6,11,256]{3,2,1,0:T(8,128)S(1)} %get-tuple-element.403), channel_id=1, source_target_pairs={{8,0},{16,8},{24,16},{0,24},{9,1},{17,9},{25,17},{1,25},{10,2},{18... | collective-permute-start | bytes 202760 | tf_op jit(solution)/shard_map/ppermute | solution.py:20
  54.2 5.8 %collective-permute-start.6 = (f32[8,1,11,256]{3,2,1,0:T(8,128)S(1)}, f32[8,1,11,256]{3,2,1,0:T(8,128)S(1)}, u32[]{:S(2)}, u32[]{:S(2)}) collective-permute-start(f32[8,1,11,256]{3,2,1,0:T(8,128)S(1)} %get-tuple-element.410), channel_id=1, source_target_pairs={{0,1},{1,2},{2,3},{3,4},{4,5},{5,6},{6,7},{7,0},{8,9},{9,10},{10,1... | collective-permute-start | bytes 270344 | tf_op jit(solution)/shard_map/ppermute | solution.py:19
  54.3 5.8 %collective-permute-start.7 = (f32[8,1,11,256]{3,2,1,0:T(8,128)S(1)}, f32[8,1,11,256]{3,2,1,0:T(8,128)S(1)}, u32[]{:S(2)}, u32[]{:S(2)}) collective-permute-start(f32[8,1,11,256]{3,2,1,0:T(8,128)S(1)} %get-tuple-element.409), channel_id=1, source_target_pairs={{1,0},{2,1},{3,2},{4,3},{5,4},{6,5},{7,6},{0,7},{9,8},{10,9},{11,1... | collective-permute-start | bytes 270344 | tf_op jit(solution)/shard_map/ppermute | solution.py:20
  65.1 0.8 copy-start.4
  65.8 0.9 slice-start.3
  69.1 7.1 %collective-permute-start.8 = (f32[1,6,11,256]{3,2,1,0:T(8,128)S(1)}, f32[1,6,11,256]{3,2,1,0:T(8,128)S(1)}, u32[]{:S(2)}, u32[]{:S(2)}) collective-permute-start(f32[1,6,11,256]{3,2,1,0:T(8,128)S(1)} %slice.1419), channel_id=1, source_target_pairs={{0,8},{8,16},{16,24},{24,0},{1,9},{9,17},{17,25},{25,1},{2,10},{10... | collective-permute-start | bytes 202760 | tf_op jit(solution)/shard_map/ppermute | solution.py:19
  76.2 4.9 %collective-permute-start.9 = (f32[1,6,11,256]{3,2,1,0:T(8,128)S(1)}, f32[1,6,11,256]{3,2,1,0:T(8,128)S(1)}, u32[]{:S(2)}, u32[]{:S(2)}) collective-permute-start(f32[1,6,11,256]{3,2,1,0:T(8,128)S(1)} %get-tuple-element.401), channel_id=1, source_target_pairs={{8,0},{16,8},{24,16},{0,24},{9,1},{17,9},{25,17},{1,25},{10,2},{18... | collective-permute-start | bytes 202760 | tf_op jit(solution)/shard_map/ppermute | solution.py:20
  81.2 6.6 %collective-permute-start.10 = (f32[8,1,11,256]{3,2,1,0:T(8,128)S(1)}, f32[8,1,11,256]{3,2,1,0:T(8,128)S(1)}, u32[]{:S(2)}, u32[]{:S(2)}) collective-permute-start(f32[8,1,11,256]{3,2,1,0:T(8,128)S(1)} %get-tuple-element.408), channel_id=1, source_target_pairs={{0,1},{1,2},{2,3},{3,4},{4,5},{5,6},{6,7},{7,0},{8,9},{9,10},{10,1... | collective-permute-start | bytes 270344 | tf_op jit(solution)/shard_map/ppermute | solution.py:19
  81.2 6.6 %collective-permute-start.11 = (f32[8,1,11,256]{3,2,1,0:T(8,128)S(1)}, f32[8,1,11,256]{3,2,1,0:T(8,128)S(1)}, u32[]{:S(2)}, u32[]{:S(2)}) collective-permute-start(f32[8,1,11,256]{3,2,1,0:T(8,128)S(1)} %get-tuple-element.407), channel_id=1, source_target_pairs={{1,0},{2,1},{3,2},{4,3},{5,4},{6,5},{7,6},{0,7},{9,8},{10,9},{11,1... | collective-permute-start | bytes 270344 | tf_op jit(solution)/shard_map/ppermute | solution.py:20
  92.0 82.8 %all-gather.2.cloned.1.call-start = ((), (), s32[]{:S(2)}) async-start(), calls=%async_computation.1 | async-start | bytes 1310720 | tf_op jit(solution)/shard_map/all_gather | solution.py:114
  (1 other events, 0.7 us)
Sparse Core Ops, SparseCore 0:
  92.1 53.6 all-reduce.19
  147.5 27.2 all-gather.1
